TPU v7x, 256 devices: a whole 4x4x8 slice. The times are simulated.
256 devices in a mesh: rows: 16 (over y_lo, z), cols: 16 (over x, y_hi, core).
Axes of the slice: x: 4, y: 4 (y_hi: 2, y_lo: 2; y = y_hi * 2 + y_lo), z: 8, core: 2. Of those that a mesh axis runs over, the one named last changes fastest.
Arguments:
- matrix: bfloat16 [4096, 32768], P('rows', 'cols'), may hold values from -0.125 to 0.125
- inverse: bfloat16 [32768, 32768], P('rows', 'cols'), may hold values from -1 to 1
- target: float32 [4096, 128], P('rows'), may hold values from -60 to 60
- penalty: float32 [128], replicated, may hold values from 0.5 to 16
- consensus: float32 [32768, 128], P('cols'), may hold values from -6 to 6
- copy_duals: float32 [16, 32768, 128], P('rows', 'cols'), may hold values from -6 to 6
- fit_parts: float32 [16, 4096, 128], P('cols', 'rows'), may hold values from -6 to 6
- fit_mean: float32 [4096, 128], P('rows'), may hold values from -3 to 3
- fit_duals: float32 [4096, 128], P('rows'), may hold values from -3 to 3
Outputs:
- coefficients: float32 [32768, 128], P('cols')
- fitted: float32 [4096, 128], P('rows')
- history: float32 [5, 2], replicated
All inputs are finite; a program needn't handle non-finite values.
Results may differ from a plain program's by a relative error of at most 0.006.
Values sent between devices are 32-bit elements; how exact they have to be, the bound alone decides.
A program may use at most 64 MiB of HBM per device.

v0:
```python
import jax
import jax.numpy as jnp
from jax import lax
from jax.sharding import Mesh
from jax.sharding import PartitionSpec as P

ITERS = 5
ROWS = ("rows_0", "rows_1")
COLS = ("cols_0", "cols_1", "cols_2")
ROWS_COLS = ("rows_0", "rows_1", "cols_0", "cols_1", "cols_2")


def sent_to_all(array, axis):
    count = lax.axis_size(axis)
    return lax.all_to_all(
        jnp.broadcast_to(array[None], (count, *array.shape)), axis, 0, 0, tiled=True
    )


def taken_together(array, axis):
    return sent_to_all(array, axis).sum(axis=0)


def gathered_total(array, axis):
    return lax.all_gather(array, axis).sum(0)


def in_blocks(array, dim, count):
    before, after = (array.shape[:dim], array.shape[dim + 1 :])
    return jnp.moveaxis(array.reshape(*before, count, -1, *after), dim, 0)


def sum_at_owner(array, axis, dim):
    count = lax.axis_size(axis)
    tiles = lax.all_to_all(in_blocks(array, dim, count), axis, 0, 0, tiled=True)
    return jnp.sum(tiles, axis=0)


def joined_along(tiles, dim):
    shape = list(tiles.shape[1:])
    shape[dim] *= tiles.shape[0]
    return jnp.moveaxis(tiles, 0, dim).reshape(shape)


def gathered_copies(array, axis, dim):
    return joined_along(sent_to_all(array, axis), dim)


def over_axes(array, axes):
    for axis in axes:
        array = lax.psum(array, axis)
    return array


def shrink(values, cutoff):
    return values - jnp.clip(values, -cutoff, cutoff)


def local(matrix, inverse, target, penalty, consensus, copy_duals, fit_parts, fit_mean, fit_duals):
    row_devices = lax.axis_size(ROWS)
    col_devices = lax.axis_size(COLS)
    block_width, targets = consensus.shape
    normalizer = float(row_devices * col_devices * block_width * targets)
    threshold = penalty / row_devices
    copy_dual = copy_duals[0]
    shares = fit_parts[0]
    mean_share = taken_together(shares, COLS) / col_devices
    center = consensus
    fitted_mean = fit_mean
    row_dual = fit_duals
    records = []
    for iteration in range(ITERS):
        offsets = (shares - mean_share + fitted_mean - row_dual).astype(jnp.bfloat16)
        pulled = lax.dot_general(
            matrix, offsets, (((0,), (0,)), ((), ())), preferred_element_type=jnp.float32
        )
        right_side = (center - copy_dual + pulled).astype(jnp.bfloat16)
        copies = jnp.dot(inverse, right_side, preferred_element_type=jnp.float32)
        shares = jnp.dot(matrix, copies.astype(jnp.bfloat16), preferred_element_type=jnp.float32)
        mean_share = gathered_total(shares, COLS) / col_devices
        summed_in = copies + copy_dual
        rows_each = block_width // row_devices
        average = sum_at_owner(summed_in, ROWS, 0) / row_devices
        first_row = lax.axis_index(ROWS) * rows_each
        old_rows = lax.dynamic_slice_in_dim(center, first_row, rows_each, 0)
        updated = shrink(average, threshold)
        motion = row_devices * jnp.sum((updated - old_rows) ** 2)
        center = gathered_copies(updated, ROWS, 0)
        fitted_mean = (target + row_dual + mean_share) / (col_devices + 1)
        spread = jnp.sum((copies - center) ** 2) + jnp.sum((mean_share - fitted_mean) ** 2)
        records.append(jnp.stack([spread, motion]))
        if iteration + 1 < ITERS:
            copy_dual = copy_dual + copies - center
            row_dual = row_dual + mean_share - fitted_mean
    history = over_axes(jnp.stack(records), ROWS_COLS) / normalizer
    return (center, fitted_mean * col_devices, history)


def solution(mesh):
    split = Mesh(
        mesh.devices.reshape(2, 8, 4, 2, 2), ("rows_0", "rows_1", "cols_0", "cols_1", "cols_2")
    )
    return jax.shard_map(
        local,
        mesh=split,
        in_specs=(
            P(ROWS, COLS),
            P(ROWS, COLS),
            P(ROWS, None),
            P(),
            P(COLS, None),
            P(ROWS, COLS, None),
            P(COLS, ROWS, None),
            P(ROWS, None),
            P(ROWS, None),
        ),
        out_specs=(P(COLS, None), P(ROWS, None), P()),
        check_vma=False,
    )
```

profile of v0, /device:TPU:1, one launch (start us, length us, event | category | flops | bytes accessed | tf_op | source)
XLA Modules:
  0.0 515.6 jit_solution(3529360706467897159)
XLA Ops:
  7.2 2.5 broadcast_in_dim.24
  9.7 8.6 %all-to-all-start = ((f32[16,256,128]{2,1,0:T(8,128)}), f32[16,256,128]{2,1,0:T(8,128)}, u32[]{:S(2)}, u32[]{:S(2)}) async-start(f32[16,256,128]{2,1,0:T(8,128)} %broadcast_in_dim.24), calls=%async_computation | async-start | bytes 4194304 | tf_op jit(solution)/shard_map/all_to_all | solution.py:15
  19.0 2.5 copy.61
  21.5 25.3 %all-to-all-done = f32[16,256,128]{2,1,0:T(8,128)} async-done(((f32[16,256,128]{2,1,0:T(8,128)}), f32[16,256,128]{2,1,0:T(8,128)}, u32[]{:S(2)}, u32[]{:S(2)}) %all-to-all-start) | async-done | bytes 2097184 | tf_op jit(solution)/shard_map/all_to_all | solution.py:15
  46.8 1.7 reduce_sum.234
  49.3 6.8 %convolution_bitcast_fusion.4 = f32[2048,128]{0,1:T(8,128)S(1)} fusion(bf16[2048,2048]{1,0:T(8,128)(2,1)} %param.10, bf16[256,2048]{1,0:T(8,128)(2,1)S(1)} %copy-done, f32[2048,128]{0,1:T(8,128)} %copy.61, f32[1,2048,128]{1,2,0:T(8,128)S(1)} %copy.60, f32[256,128]{0,1:T(8,128)S(1)} %copy.66, f32[256,128]{0,1:T(8,128)S(1)} %copy.65, ...), kind=kOutput, calls=%fused_computation.4 | convolution fusion | flops 1208909824 | bytes 13107200 | tf_op jit(solution)/shard_map/dot_general | solution.py:78
  56.1 1.1 copy_bitcast_fusion.9
  57.3 8.6 %all-to-all-start.1 = ((f32[16,128,128]{1,2,0:T(8,128)}), f32[16,128,128]{1,2,0:T(8,128)}, u32[]{:S(2)}, u32[]{:S(2)}) async-start(f32[16,128,128]{1,2,0:T(8,128)} %copy_bitcast_fusion.9), calls=%async_computation.1 | async-start | bytes 2097152 | tf_op jit(solution)/shard_map/all_to_all | solution.py:35
  65.9 1.1 convolution_bitcast_fusion.14
  67.1 24.2 %all-to-all-done.1 = f32[16,128,128]{1,2,0:T(8,128)} async-done(((f32[16,128,128]{1,2,0:T(8,128)}), f32[16,128,128]{1,2,0:T(8,128)}, u32[]{:S(2)}, u32[]{:S(2)}) %all-to-all-start.1) | async-done | bytes 1048608 | tf_op jit(solution)/shard_map/all_to_all | solution.py:35
  91.3 1.3 reduce_sum.235
  92.6 1.6 multiply_reduce_fusion.14
  95.2 6.3 %all-to-all-start.2 = ((f32[16,128,128]{1,2,0:T(8,128)}), f32[16,128,128]{1,2,0:T(8,128)}, u32[]{:S(2)}, u32[]{:S(2)}) async-start(f32[16,128,128]{1,2,0:T(8,128)} %broadcast_in_dim.25), calls=%async_computation.2 | async-start | bytes 2097152 | tf_op jit(solution)/shard_map/all_to_all | solution.py:15
  101.6 29.3 %all-gather.11.cloned.1.call-done = f32[4096,128]{0,1:T(8,128)} async-done(((f32[256,128]{0,1:T(8,128)}), f32[4096,128]{0,1:T(8,128)}) %all-gather.11.cloned.1.call-update) | async-done | bytes 2097168 | tf_op jit(solution)/shard_map/all_gather | solution.py:25
  130.9 2.3 copy.103
  133.6 9.2 %multiply_reduce_fusion.4 = (f32[]{:T(128)}, f32[2048,128]{0,1:T(8,128)}, f32[2048,128]{0,1:T(8,128)}) fusion(f32[2048,128]{0,1:T(8,128)S(1)} %convolution_bitcast_fusion.4, f32[1,2048,128]{1,2,0:T(8,128)S(1)} %copy.60, bf16[2048,2048]{1,0:T(8,128)(2,1)} %param.10, bf16[256,2048]{1,0:T(8,128)(2,1)S(1)} %copy-done, ...), kind=kOutput, calls=%fused_computation.46 | convolution fusion | flops 1211170816 | bytes 15204356 | tf_op jit(solution)/shard_map/dot_general | solution.py:78
  142.7 2.4 copy_bitcast_fusion.8
  145.1 5.2 %all-to-all-start.3 = ((f32[16,128,128]{1,2,0:T(8,128)}), f32[16,128,128]{1,2,0:T(8,128)S(1)}, u32[]{:S(2)}, u32[]{:S(2)}) async-start(f32[16,128,128]{1,2,0:T(8,128)} %copy_bitcast_fusion.8), calls=%async_computation.3 | async-start | bytes 2097152 | tf_op jit(solution)/shard_map/all_to_all | solution.py:35
  150.3 1.1 convolution_bitcast_fusion.13
  151.5 1.3 copy_bitcast_fusion.4
  152.8 22.9 %all-to-all-done.3 = f32[16,128,128]{1,2,0:T(8,128)S(1)} async-done(((f32[16,128,128]{1,2,0:T(8,128)}), f32[16,128,128]{1,2,0:T(8,128)S(1)}, u32[]{:S(2)}, u32[]{:S(2)}) %all-to-all-start.3) | async-done | bytes 1048608 | tf_op jit(solution)/shard_map/all_to_all | solution.py:35
  176.4 1.6 multiply_reduce_fusion.13
  178.0 1.1 broadcast_in_dim.26
  179.1 6.2 %all-to-all-start.4 = ((f32[16,128,128]{1,2,0:T(8,128)}), f32[16,128,128]{1,2,0:T(8,128)S(1)}, u32[]{:S(2)}, u32[]{:S(2)}) async-start(f32[16,128,128]{1,2,0:T(8,128)} %broadcast_in_dim.26), calls=%async_computation.4 | async-start | bytes 2097152 | tf_op jit(solution)/shard_map/all_to_all | solution.py:15
  185.6 30.7 %all-gather.13.cloned.1.call-done = f32[4096,128]{0,1:T(8,128)} async-done(((f32[256,128]{0,1:T(8,128)}), f32[4096,128]{0,1:T(8,128)}) %all-gather.13.cloned.1.call-update) | async-done | bytes 2097168 | tf_op jit(solution)/shard_map/all_gather | solution.py:25
  216.2 2.3 copy.104
  219.7 8.9 %multiply_reduce_fusion.3 = (f32[]{:T(128)}, f32[2048,128]{0,1:T(8,128)}, f32[2048,128]{0,1:T(8,128)}) fusion(f32[2048,128]{0,1:T(8,128)} %get-tuple-element.41, f32[2048,128]{0,1:T(8,128)S(1)} %copy-done.1, bf16[2048,2048]{1,0:T(8,128)(2,1)} %param.10, bf16[256,2048]{1,0:T(8,128)(2,1)S(1)} %copy-done, f32[256,128]{0,1:T(8,128)} %convolution_bitcast_fusion.13, ...), kind=kOutput, calls=%fused_computation.45 | convolution fusion | flops 1210843136 | bytes 15335428 | tf_op jit(solution)/shard_map/dot_general | solution.py:78
  228.6 2.5 convolution_bitcast_fusion.12
  231.1 1.1 copy_bitcast_fusion.7
  232.2 8.2 %all-to-all-start.5 = ((f32[16,128,128]{1,2,0:T(8,128)}), f32[16,128,128]{1,2,0:T(8,128)S(1)}, u32[]{:S(2)}, u32[]{:S(2)}) async-start(f32[16,128,128]{1,2,0:T(8,128)} %copy_bitcast_fusion.7), calls=%async_computation.5 | async-start | bytes 2097152 | tf_op jit(solution)/shard_map/all_to_all | solution.py:35
  241.5 24.4 %all-to-all-done.5 = f32[16,128,128]{1,2,0:T(8,128)S(1)} async-done(((f32[16,128,128]{1,2,0:T(8,128)}), f32[16,128,128]{1,2,0:T(8,128)S(1)}, u32[]{:S(2)}, u32[]{:S(2)}) %all-to-all-start.5) | async-done | bytes 1048608 | tf_op jit(solution)/shard_map/all_to_all | solution.py:35
  265.9 1.6 multiply_reduce_fusion.12
  268.5 6.2 %all-to-all-start.6 = ((f32[16,128,128]{1,2,0:T(8,128)}), f32[16,128,128]{1,2,0:T(8,128)S(1)}, u32[]{:S(2)}, u32[]{:S(2)}) async-start(f32[16,128,128]{1,2,0:T(8,128)} %broadcast_in_dim.50), calls=%async_computation.6 | async-start | bytes 2097152 | tf_op jit(solution)/shard_map/all_to_all | solution.py:15
  274.8 9.9 %all-gather.15.cloned.1.call-done = f32[4096,128]{0,1:T(8,128)} async-done(((f32[256,128]{0,1:T(8,128)}), f32[4096,128]{0,1:T(8,128)}) %all-gather.15.cloned.1.call-update) | async-done | bytes 2097168 | tf_op jit(solution)/shard_map/all_gather | solution.py:25
  284.7 2.3 copy.105
  288.6 11.7 %all-to-all-done.6 = f32[16,128,128]{1,2,0:T(8,128)S(1)} async-done(((f32[16,128,128]{1,2,0:T(8,128)}), f32[16,128,128]{1,2,0:T(8,128)S(1)}, u32[]{:S(2)}, u32[]{:S(2)}) %all-to-all-start.6) | async-done | bytes 1048608 | tf_op jit(solution)/shard_map/all_to_all | solution.py:15
  300.2 9.2 %multiply_reduce_fusion.2 = (f32[]{:T(128)}, f32[2048,128]{0,1:T(8,128)S(1)}, f32[2048,128]{0,1:T(8,128)}) fusion(f32[2048,128]{0,1:T(8,128)} %get-tuple-element.42, f32[2048,128]{0,1:T(8,128)} %get-tuple-element.37, bf16[2048,2048]{1,0:T(8,128)(2,1)} %param.10, bf16[256,2048]{1,0:T(8,128)(2,1)S(1)} %copy-done, f32[256,128]{0,1:T(8,128)} %add_subtract_fusion.1, ...), kind=kOutput, calls=%fused_computation.44 | convolution fusion | flops 1210974208 | bytes 15597572 | tf_op jit(solution)/shard_map/dot_general | solution.py:78
  310.5 6.2 %all-to-all-start.7 = ((f32[16,128,128]{1,2,0:T(8,128)}), f32[16,128,128]{1,2,0:T(8,128)}, u32[]{:S(2)}, u32[]{:S(2)}) async-start(f32[16,128,128]{1,2,0:T(8,128)} %copy_bitcast_fusion.6), calls=%async_computation.7 | async-start | bytes 2097152 | tf_op jit(solution)/shard_map/all_to_all | solution.py:35
  316.8 2.4 convolution_bitcast_fusion.11
  320.3 22.0 %all-to-all-done.7 = f32[16,128,128]{1,2,0:T(8,128)} async-done(((f32[16,128,128]{1,2,0:T(8,128)}), f32[16,128,128]{1,2,0:T(8,128)}, u32[]{:S(2)}, u32[]{:S(2)}) %all-to-all-start.7) | async-done | bytes 1048608 | tf_op jit(solution)/shard_map/all_to_all | solution.py:35
  342.3 1.3 reduce_sum.241
  343.6 1.6 multiply_reduce_fusion.11
  346.3 6.2 %all-to-all-start.8 = ((f32[16,128,128]{1,2,0:T(8,128)}), f32[16,128,128]{1,2,0:T(8,128)}, u32[]{:S(2)}, u32[]{:S(2)}) async-start(f32[16,128,128]{1,2,0:T(8,128)} %broadcast_in_dim.51), calls=%async_computation.8 | async-start | bytes 2097152 | tf_op jit(solution)/shard_map/all_to_all | solution.py:15
  352.8 26.6 %all-gather.17.cloned.1.call-done = f32[4096,128]{0,1:T(8,128)} async-done(((f32[256,128]{0,1:T(8,128)}), f32[4096,128]{0,1:T(8,128)}) %all-gather.17.cloned.1.call-update) | async-done | bytes 2097168 | tf_op jit(solution)/shard_map/all_gather | solution.py:25
  379.4 2.3 copy.106
  382.7 7.0 %convolution_bitcast_fusion = f32[2048,128]{0,1:T(8,128)S(1)} fusion(bf16[2048,2048]{1,0:T(8,128)(2,1)} %param.10, bf16[256,2048]{1,0:T(8,128)(2,1)S(1)} %copy-done, f32[2048,128]{0,1:T(8,128)S(1)} %get-tuple-element.35, f32[256,128]{0,1:T(8,128)} %convolution_bitcast_fusion.11, f32[256,128]{0,1:T(8,128)} %bitcast_reduce_fusion.1, ...), kind=kOutput, calls=%fused_computation | convolution fusion | flops 1209335808 | bytes 13107200 | tf_op jit(solution)/shard_map/dot_general | solution.py:78
  389.6 1.1 convolution_bitcast_fusion.10
  390.8 2.4 multiply_reduce_fusion.1
  393.3 1.1 copy.154
  394.4 5.5 %all-to-all-start.9 = ((f32[16,128,128]{1,2,0:T(8,128)}), f32[16,128,128]{1,2,0:T(8,128)S(1)}, u32[]{:S(2)}, u32[]{:S(2)}) async-start(f32[16,128,128]{1,2,0:T(8,128)} %bitcast.258), calls=%async_computation.9 | async-start | bytes 2097152 | tf_op jit(solution)/shard_map/all_to_all | solution.py:35
  399.8 2.3 copy_bitcast_fusion.1
  402.1 23.1 %all-to-all-done.9 = f32[16,128,128]{1,2,0:T(8,128)S(1)} async-done(((f32[16,128,128]{1,2,0:T(8,128)}), f32[16,128,128]{1,2,0:T(8,128)S(1)}, u32[]{:S(2)}, u32[]{:S(2)}) %all-to-all-start.9) | async-done | bytes 1048608 | tf_op jit(solution)/shard_map/all_to_all | solution.py:35
  425.9 1.6 multiply_reduce_fusion.10
  428.6 6.3 %all-to-all-start.10 = ((f32[16,128,128]{1,2,0:T(8,128)}), f32[16,128,128]{1,2,0:T(8,128)S(1)}, u32[]{:S(2)}, u32[]{:S(2)}) async-start(f32[16,128,128]{1,2,0:T(8,128)} %broadcast_in_dim.52), calls=%async_computation.10 | async-start | bytes 2097152 | tf_op jit(solution)/shard_map/all_to_all | solution.py:15
  438.0 7.2 %all-gather.19.cloned.1.call-done = f32[4096,128]{0,1:T(8,128)} async-done(((f32[256,128]{0,1:T(8,128)}), f32[4096,128]{0,1:T(8,128)}) %all-gather.19.cloned.1.call-update) | async-done | bytes 2097168 | tf_op jit(solution)/shard_map/all_gather | solution.py:25
  445.2 2.3 copy.107
  448.6 1.5 multiply_reduce_fusion.5
  455.7 4.6 all-to-all-done.10
  462.8 3.8 psum.35
  466.6 12.1 %psum.36 = f32[5,2]{0,1:T(2,128)S(1)} all-reduce(f32[5,2]{0,1:T(2,128)S(1)} %psum.35), channel_id=1, replica_groups=mesh['rows_0'=2,'rows_1'=8,'cols_0'=4,'cols_1'=2,'cols_2'=2] {'rows_1'}, use_global_device_ids=true, to_apply=%region_27.28 | all-reduce | flops 10 | bytes 80 | tf_op jit(solution)/shard_map/psum | solution.py:51
  478.7 10.3 %psum.37 = f32[5,2]{0,1:T(2,128)S(1)} all-reduce(f32[5,2]{0,1:T(2,128)S(1)} %psum.36), channel_id=1, replica_groups=mesh['rows_0'=2,'rows_1'=8,'cols_0'=4,'cols_1'=2,'cols_2'=2] {'cols_0'}, use_global_device_ids=true, to_apply=%region_28.29 | all-reduce | flops 10 | bytes 80 | tf_op jit(solution)/shard_map/psum | solution.py:51
  489.8 5.3 %psum.38 = f32[5,2]{0,1:T(2,128)S(1)} all-reduce(f32[5,2]{0,1:T(2,128)S(1)} %psum.37), channel_id=1, replica_groups=mesh['rows_0'=2,'rows_1'=8,'cols_0'=4,'cols_1'=2,'cols_2'=2] {'cols_1'}, use_global_device_ids=true, to_apply=%region_29.30 | all-reduce | flops 10 | bytes 80 | tf_op jit(solution)/shard_map/psum | solution.py:51
  495.1 1.3 copy.90
  496.4 12.0 %psum.39 = f32[5,2]{0,1:T(2,128)S(1)} all-reduce(f32[5,2]{0,1:T(2,128)S(1)} %psum.38), channel_id=1, replica_groups=mesh['rows_0'=2,'rows_1'=8,'cols_0'=4,'cols_1'=2,'cols_2'=2] {'cols_2'}, use_global_device_ids=true, to_apply=%region_30.31 | all-reduce | flops 10 | bytes 80 | tf_op jit(solution)/shard_map/psum | solution.py:51
  (85 shorter events, 19.6 us)
Async XLA Ops:
  7.2 42.1 %copy-start = (bf16[256,2048]{1,0:T(8,128)(2,1)S(1)}, bf16[256,2048]{1,0:T(8,128)(2,1)}, u32[]{:S(2)}) copy-start(bf16[256,2048]{1,0:T(8,128)(2,1)} %param.9) | copy-start | bytes 3145732
  9.7 8.6 %copy-start.11 = (f32[1,256,128]{2,1,0:T(8,128)S(1)}, f32[1,256,128]{2,1,0:T(8,128)}, u32[]{:S(2)}) copy-start(f32[1,256,128]{2,1,0:T(8,128)} %param.15) | copy-start | bytes 393220
  9.7 8.7 %copy-start.13 = (f32[256,128]{1,0:T(8,128)S(1)}, f32[256,128]{1,0:T(8,128)}, u32[]{:S(2)}) copy-start(f32[256,128]{1,0:T(8,128)} %param.17) | copy-start | bytes 393220
  9.7 8.8 %copy-start.14 = (f32[256,128]{1,0:T(8,128)S(1)}, f32[256,128]{1,0:T(8,128)}, u32[]{:S(2)}) copy-start(f32[256,128]{1,0:T(8,128)} %param.16) | copy-start | bytes 393220
  9.7 8.9 %copy-start.10 = (f32[1,2048,128]{2,1,0:T(8,128)S(1)}, f32[1,2048,128]{2,1,0:T(8,128)}, u32[]{:S(2)}) copy-start(f32[1,2048,128]{2,1,0:T(8,128)} %param.14) | copy-start | bytes 3145732
  9.7 37.1 %all-to-all-start = ((f32[16,256,128]{2,1,0:T(8,128)}), f32[16,256,128]{2,1,0:T(8,128)}, u32[]{:S(2)}, u32[]{:S(2)}) async-start(f32[16,256,128]{2,1,0:T(8,128)} %broadcast_in_dim.24), calls=%async_computation | async-start | bytes 4194304 | tf_op jit(solution)/shard_map/all_to_all | solution.py:15
  57.2 9.8 %copy-start.16 = (f32[128]{0:T(128)S(1)}, f32[128]{0:T(128)}, u32[]{:S(2)}) copy-start(f32[128]{0:T(128)} %param.12) | copy-start | bytes 1540
  57.3 34.1 %all-to-all-start.1 = ((f32[16,128,128]{1,2,0:T(8,128)}), f32[16,128,128]{1,2,0:T(8,128)}, u32[]{:S(2)}, u32[]{:S(2)}) async-start(f32[16,128,128]{1,2,0:T(8,128)} %copy_bitcast_fusion.9), calls=%async_computation.1 | async-start | bytes 2097152 | tf_op jit(solution)/shard_map/all_to_all | solution.py:35
  65.8 65.1 %all-gather.11.cloned.1.call-start = ((), (), s32[]{:S(2)}) async-start(), calls=%async_computation.11 | async-start | bytes 2228224 | tf_op jit(solution)/shard_map/all_gather | solution.py:25
  67.1 34.4 %copy-start.15 = (f32[256,128]{1,0:T(8,128)S(1)}, f32[256,128]{1,0:T(8,128)}, u32[]{:S(2)}) copy-start(f32[256,128]{1,0:T(8,128)} %param.11) | copy-start | bytes 393220
  95.2 38.3 %all-to-all-start.2 = ((f32[16,128,128]{1,2,0:T(8,128)}), f32[16,128,128]{1,2,0:T(8,128)}, u32[]{:S(2)}, u32[]{:S(2)}) async-start(f32[16,128,128]{1,2,0:T(8,128)} %broadcast_in_dim.25), calls=%async_computation.2 | async-start | bytes 2097152 | tf_op jit(solution)/shard_map/all_to_all | solution.py:15
  142.7 7.6 %copy-start.2 = (f32[2048,128]{0,1:T(8,128)S(1)}, f32[2048,128]{0,1:T(8,128)}, u32[]{:S(2)}) copy-start(f32[2048,128]{0,1:T(8,128)} %get-tuple-element.41) | copy-start | bytes 3145732
  145.1 30.6 %all-to-all-start.3 = ((f32[16,128,128]{1,2,0:T(8,128)}), f32[16,128,128]{1,2,0:T(8,128)S(1)}, u32[]{:S(2)}, u32[]{:S(2)}) async-start(f32[16,128,128]{1,2,0:T(8,128)} %copy_bitcast_fusion.8), calls=%async_computation.3 | async-start | bytes 2097152 | tf_op jit(solution)/shard_map/all_to_all | solution.py:35
  150.3 66.0 %all-gather.13.cloned.1.call-start = ((), (), s32[]{:S(2)}) async-start(), calls=%async_computation.12 | async-start | bytes 2228224 | tf_op jit(solution)/shard_map/all_gather | solution.py:25
  179.1 40.4 %all-to-all-start.4 = ((f32[16,128,128]{1,2,0:T(8,128)}), f32[16,128,128]{1,2,0:T(8,128)S(1)}, u32[]{:S(2)}, u32[]{:S(2)}) async-start(f32[16,128,128]{1,2,0:T(8,128)} %broadcast_in_dim.26), calls=%async_computation.4 | async-start | bytes 2097152 | tf_op jit(solution)/shard_map/all_to_all | solution.py:15
  185.3 99.3 %all-gather.15.cloned.1.call-start = ((), (), s32[]{:S(2)}) async-start(), calls=%async_computation.13 | async-start | bytes 2228224 | tf_op jit(solution)/shard_map/all_gather | solution.py:25
  218.5 1.2 copy-start.1
  228.6 2.5 copy-start.3
  232.2 33.7 %all-to-all-start.5 = ((f32[16,128,128]{1,2,0:T(8,128)}), f32[16,128,128]{1,2,0:T(8,128)S(1)}, u32[]{:S(2)}, u32[]{:S(2)}) async-start(f32[16,128,128]{1,2,0:T(8,128)} %copy_bitcast_fusion.7), calls=%async_computation.5 | async-start | bytes 2097152 | tf_op jit(solution)/shard_map/all_to_all | solution.py:35
  268.5 31.7 %all-to-all-start.6 = ((f32[16,128,128]{1,2,0:T(8,128)}), f32[16,128,128]{1,2,0:T(8,128)S(1)}, u32[]{:S(2)}, u32[]{:S(2)}) async-start(f32[16,128,128]{1,2,0:T(8,128)} %broadcast_in_dim.50), calls=%async_computation.6 | async-start | bytes 2097152 | tf_op jit(solution)/shard_map/all_to_all | solution.py:15
  286.9 0.9 copy-start.4
  287.8 0.8 copy-start.7
  310.5 31.8 %all-to-all-start.7 = ((f32[16,128,128]{1,2,0:T(8,128)}), f32[16,128,128]{1,2,0:T(8,128)}, u32[]{:S(2)}, u32[]{:S(2)}) async-start(f32[16,128,128]{1,2,0:T(8,128)} %copy_bitcast_fusion.6), calls=%async_computation.7 | async-start | bytes 2097152 | tf_op jit(solution)/shard_map/all_to_all | solution.py:35
  316.8 62.7 %all-gather.17.cloned.1.call-start = ((), (), s32[]{:S(2)}) async-start(), calls=%async_computation.14 | async-start | bytes 2228224 | tf_op jit(solution)/shard_map/all_gather | solution.py:25
  346.3 36.4 %all-to-all-start.8 = ((f32[16,128,128]{1,2,0:T(8,128)}), f32[16,128,128]{1,2,0:T(8,128)}, u32[]{:S(2)}, u32[]{:S(2)}) async-start(f32[16,128,128]{1,2,0:T(8,128)} %broadcast_in_dim.51), calls=%async_computation.8 | async-start | bytes 2097152 | tf_op jit(solution)/shard_map/all_to_all | solution.py:15
  352.5 92.7 %all-gather.19.cloned.1.call-start = ((), (), s32[]{:S(2)}) async-start(), calls=%async_computation.15 | async-start | bytes 2228224 | tf_op jit(solution)/shard_map/all_gather | solution.py:25
  394.4 30.9 %all-to-all-start.9 = ((f32[16,128,128]{1,2,0:T(8,128)}), f32[16,128,128]{1,2,0:T(8,128)S(1)}, u32[]{:S(2)}, u32[]{:S(2)}) async-start(f32[16,128,128]{1,2,0:T(8,128)} %bitcast.258), calls=%async_computation.9 | async-start | bytes 2097152 | tf_op jit(solution)/shard_map/all_to_all | solution.py:35
  428.6 31.8 %all-to-all-start.10 = ((f32[16,128,128]{1,2,0:T(8,128)}), f32[16,128,128]{1,2,0:T(8,128)S(1)}, u32[]{:S(2)}, u32[]{:S(2)}) async-start(f32[16,128,128]{1,2,0:T(8,128)} %broadcast_in_dim.52), calls=%async_computation.10 | async-start | bytes 2097152 | tf_op jit(solution)/shard_map/all_to_all | solution.py:15
  447.5 0.9 copy-start.5
  447.5 1.0 copy-start.6
  447.5 1.0 copy-start.8
  447.5 1.1 copy-start.9
  450.1 38.9 %copy-start.12 = (f32[256,128]{0,1:T(8,128)S(1)}, f32[256,128]{0,1:T(8,128)}, u32[]{:S(2)}) copy-start(f32[256,128]{0,1:T(8,128)} %get-tuple-element.38) | copy-start | bytes 393220
Sparse Core Ops, SparseCore 0:
  69.8 61.0 all-gather.10
  154.2 61.9 all-gather.12
  231.2 53.4 all-gather.14
  320.4 58.9 all-gather.16
  390.9 54.2 all-gather.18
where the time goes:
time: 518 us; the launch traced here: 516 us
  waiting for transfers between devices  262 us (51%)
  starting transfers between devices  74.1 us (14%)
  matrix products  49.3 us (10%)
  blocking collectives  43.5 us (8%)
  local copies, waits for them, and re-layouts  38.9 us (8%)
  other arithmetic  24.3 us (5%)
  between operations  23.6 us (5%)
    all_to_all x5, waiting for transfers between devices, sum_at_owner(): tiles = lax.all_to_all(in_blocks(array, dim, count), axis, 0, 0, tiled=True)  117 us
    all_gather x5, waiting for transfers between devices, gathered_total(): return lax.all_gather(array, axis).sum(0)  104 us
    psum x5, blocking collectives, over_axes(): array = lax.psum(array, axis)  43.5 us
    all_to_all x6, waiting for transfers between devices, sent_to_all(): lax.all_to_all(jnp.broadcast_to(array[None], (count, *array.shape)), axis...  41.6 us
    dot_general x5, matrix products, local(): copies = jnp.dot(inverse, right_side, preferred_element_type=jnp.float32)  41 us
    all_to_all x6, starting transfers between devices, sent_to_all(): lax.all_to_all(jnp.broadcast_to(array[None], (count, *array.shape)), axis...  39.9 us
    all_to_all x5, starting transfers between devices, sum_at_owner(): tiles = lax.all_to_all(in_blocks(array, dim, count), axis, 0, 0, tiled=True)  33.7 us
    unnamed x47, local copies, waits for them, and re-layouts  18.1 us
  transfers between devices with their start and end apart: 16, of which 13 were waited for; matrix products, arithmetic and copies ran while one was open for 10% of the time, Pallas kernels for 0%

commit v1 on v0

v1 whole, which is shorter than its diff:
```python
import jax
import jax.numpy as jnp
from jax import lax
from jax.experimental import pallas as pl
from jax.experimental.pallas import tpu as pltpu
from jax.sharding import Mesh
from jax.sharding import PartitionSpec as P

ITERS = 5
ROWS = ("rows_0", "rows_1")
COLS = ("cols_0", "cols_1", "cols_2")
AXES = ("rows_0", "rows_1", "cols_0", "cols_1", "cols_2")
SIZES = (2, 8, 4, 2, 2)
MESH = pl.DeviceIdType.MESH

WIDTH = 2048
HEIGHT = 256
TARGETS = 128
NZ = 8
CHUNKS = 4
CHUNK = WIDTH // CHUNKS
PIECE = CHUNK // NZ
HALF = HEIGHT // 2
QUARTER = HALF // 4
LOADS = 9
NORMALIZER = 16.0 * 32768.0 * 128.0


def kernel(
    inverse_hbm, matrix_hbm, target_hbm, penalty_ref, consensus_hbm, duals_hbm, parts_hbm, mean_hbm, fit_duals_hbm,
    coef_hbm, fitted_ref, history_ref,
    cache, tile, tile_t, center, dual, summed, copies, pulled, right_side, rounded,
    share, share_mean, fitted_mean, row_dual, observed,
    chain, y_out, y_in, core_in, x_in, half_sum, quarter_sum, yh_in, record, record_in,
    load_sem, cache_sem, store_sem,
    rs_send, rs_recv, ag_send, ag_recv, y_send, y_recv, s_send, s_recv, h_send, h_recv,
):
    me = tuple(lax.axis_index(axis) for axis in AXES)
    my_y, my_z, my_x, my_yh, my_core = me

    def device(**moved):
        return tuple(moved.get(axis, index) for axis, index in zip(AXES, me))

    def z_at(offset):
        return lax.rem(my_z + offset + 2 * NZ, NZ)

    core_peer = device(cols_2=1 - my_core)
    yh_peer = device(cols_1=1 - my_yh)
    y_peer = device(rows_0=1 - my_y)

    def x_peer(step):
        return device(cols_0=lax.rem(my_x + step, 4))

    peers = [core_peer, yh_peer, y_peer]
    peers += [x_peer(step) for step in range(1, 4)]
    peers += [device(rows_1=z_at(step)) for step in range(1, NZ)]
    barrier = pltpu.get_barrier_semaphore()
    for peer in peers:
        pl.semaphore_signal(barrier, inc=1, device_id=peer, device_id_type=MESH)

    loads = [
        pltpu.make_async_copy(src, dst, load_sem.at[index])
        for index, (src, dst) in enumerate(
            (
                (parts_hbm.at[0], share),
                (matrix_hbm, tile),
                (mean_hbm, fitted_mean),
                (fit_duals_hbm, row_dual),
                (consensus_hbm, center.at[1]),
                (duals_hbm.at[0], dual),
                (target_hbm, observed),
            )
        )
    ]
    for load in loads:
        load.start()

    def cache_load(chunk):
        rows = pl.ds(chunk * CHUNK, CHUNK)
        return pltpu.make_async_copy(inverse_hbm.at[rows], cache.at[rows], cache_sem.at[chunk])

    for chunk in range(CHUNKS):
        cache_load(chunk).start()

    def remote(src, dst, send, recv, where):
        return pltpu.make_async_remote_copy(
            src_ref=src, dst_ref=dst, send_sem=send, recv_sem=recv, device_id=where, device_id_type=MESH
        )

    mine = pl.ds(my_core * HALF, HALF)
    other = pl.ds((1 - my_core) * HALF, HALF)

    def quarter(x_index):
        return pl.ds(x_index * QUARTER, QUARTER)

    def piece_of_mean(x_index):
        return pl.ds(my_core * HALF + x_index * QUARTER, QUARTER)

    def core_sum(par):
        return remote(share.at[other], core_in.at[par], s_send.at[par, 0], s_recv.at[par, 0], core_peer)

    def x_sum(par, step):
        return remote(
            half_sum.at[quarter(lax.rem(my_x + step, 4))], x_in.at[par, step - 1],
            s_send.at[par, step], s_recv.at[par, step], x_peer(step),
        )

    def yh_sum(par):
        return remote(quarter_sum, yh_in.at[par], s_send.at[par, 4], s_recv.at[par, 4], yh_peer)

    def x_copy(par, step):
        return remote(
            share_mean.at[par, piece_of_mean(my_x)], share_mean.at[par, piece_of_mean(my_x)],
            s_send.at[par, 4 + step], s_recv.at[par, 4 + step], x_peer(step),
        )

    def core_copy(par):
        return remote(
            share_mean.at[par, mine], share_mean.at[par, mine], s_send.at[par, 8], s_recv.at[par, 8], core_peer
        )

    def stage_a(par):
        core_sum(par).start()

    def stage_b(par):
        core_sum(par).wait()
        half_sum[...] = share[mine, :] + core_in[par]
        for step in range(1, 4):
            x_sum(par, step).start()

    def stage_c(par):
        for step in range(1, 4):
            x_sum(par, step).wait()
        quarter_sum[...] = half_sum[quarter(my_x), :] + (x_in[par, 0] + x_in[par, 1] + x_in[par, 2])
        yh_sum(par).start()

    def stage_d(par):
        yh_sum(par).wait()
        share_mean[par, piece_of_mean(my_x), :] = (quarter_sum[...] + yh_in[par]) * (1.0 / 16)
        for step in range(1, 4):
            x_copy(par, step).start()

    def stage_e(par):
        for step in range(1, 4):
            x_copy(par, step).wait()
        core_copy(par).start()

    def stage_f(par):
        core_copy(par).wait()

    def pull(par):
        offsets = (share[...] - share_mean[par] + fitted_mean[...] - row_dual[...]).astype(jnp.bfloat16)
        pulled[...] = jnp.dot(tile_t[...], offsets, preferred_element_type=jnp.float32)

    loads[0].wait()
    pl.semaphore_wait(barrier, len(peers))
    stage_a(1)
    loads[1].wait()
    for block in range(WIDTH // HEIGHT):
        columns = slice(block * HEIGHT, (block + 1) * HEIGHT)
        tile_t[columns, :] = tile[:, columns].T
    stage_b(1)
    for load in loads[2:]:
        load.wait()
    record[...] = jnp.zeros_like(record)
    stage_c(1)
    stage_d(1)
    stage_e(1)
    stage_f(1)
    pull(1)
    for chunk in range(CHUNKS):
        rows = slice(chunk * CHUNK, (chunk + 1) * CHUNK)
        right_side[rows, :] = (center[1, rows, :] - dual[rows, :] + pulled[rows, :]).astype(jnp.bfloat16)
    threshold = penalty_ref[...] * (1.0 / 16)
    for chunk in range(CHUNKS):
        cache_load(chunk).wait()

    def turn(chunk):
        return 1 - 2 * lax.rem(chunk, 2)

    def piece(chunk, z_index):
        return pl.ds(pl.multiple_of(chunk * CHUNK + z_index * PIECE, PIECE), PIECE)

    def along(chunk, sign):
        return device(rows_1=z_at(sign * turn(chunk)))

    def first_hop(par, chunk, sign):
        slot, far = (0, 4) if sign > 0 else (4, -3)
        return remote(
            summed.at[piece(chunk, z_at(far * turn(chunk)))], chain.at[par, chunk, slot],
            rs_send.at[par, chunk, slot], rs_recv.at[par, chunk, slot], along(chunk, sign),
        )

    def next_hop(par, chunk, slot, sign):
        return remote(
            chain.at[par, chunk, slot - 1], chain.at[par, chunk, slot],
            rs_send.at[par, chunk, slot], rs_recv.at[par, chunk, slot], along(chunk, sign),
        )

    def add_here(par, chunk, slot, offset):
        chain[par, chunk, slot] = chain[par, chunk, slot] + summed[piece(chunk, z_at(offset * turn(chunk))), :]

    def y_swap(par, chunk):
        return remote(y_out.at[par, chunk], y_in.at[par, chunk], y_send.at[par, chunk], y_recv.at[par, chunk], y_peer)

    def spread_hop(par, chunk, hop, sign):
        slot = hop if sign > 0 else 4 + hop
        where = piece(chunk, z_at(-sign * hop * turn(chunk)))
        return remote(
            center.at[par, where], center.at[par, where],
            ag_send.at[par, chunk, slot], ag_recv.at[par, chunk, slot], along(chunk, sign),
        )

    def each_chunk(body):
        def step(chunk, carry):
            body(chunk)
            return carry

        lax.fori_loop(0, CHUNKS, step, 0)

    def in_rows(values):
        return jnp.sum(values.reshape(-1, 8, TARGETS), axis=0)

    def iteration(k, carry):
        par = lax.rem(k, 2)
        old = 1 - par

        def multiply(chunk):
            rows = pl.ds(pl.multiple_of(chunk * CHUNK, CHUNK), CHUNK)
            product = jnp.dot(cache[rows, :], right_side[...], preferred_element_type=jnp.float32)
            copies[rows, :] = product
            rounded[rows, :] = product.astype(jnp.bfloat16)
            summed[rows, :] = product + dual[rows, :]
            first_hop(par, chunk, 1).start()
            first_hop(par, chunk, -1).start()

        each_chunk(multiply)
        share[...] = jnp.dot(tile[...], rounded[...], preferred_element_type=jnp.float32)
        stage_a(par)

        def second(chunk):
            first_hop(par, chunk, 1).wait_recv()
            add_here(par, chunk, 0, 3)
            next_hop(par, chunk, 1, 1).start()
            first_hop(par, chunk, -1).wait_recv()
            add_here(par, chunk, 4, -2)
            next_hop(par, chunk, 5, -1).start()

        each_chunk(second)
        stage_b(par)

        def third(chunk):
            next_hop(par, chunk, 1, 1).wait_recv()
            add_here(par, chunk, 1, 2)
            next_hop(par, chunk, 2, 1).start()
            next_hop(par, chunk, 5, -1).wait_recv()
            add_here(par, chunk, 5, -1)
            next_hop(par, chunk, 6, -1).start()

        each_chunk(third)
        stage_c(par)

        def fourth(chunk):
            next_hop(par, chunk, 2, 1).wait_recv()
            add_here(par, chunk, 2, 1)
            next_hop(par, chunk, 3, 1).start()

        each_chunk(fourth)
        stage_d(par)

        def owned(chunk):
            next_hop(par, chunk, 6, -1).wait_recv()
            next_hop(par, chunk, 3, 1).wait_recv()
            y_out[par, chunk] = summed[piece(chunk, my_z), :] + (chain[par, chunk, 3] + chain[par, chunk, 6])
            y_swap(par, chunk).start()

        each_chunk(owned)
        stage_e(par)

        def update(chunk, motion):
            y_swap(par, chunk).wait_recv()
            average = (y_out[par, chunk] + y_in[par, chunk]) * (1.0 / 16)
            updated = average - jnp.clip(average, -threshold, threshold)
            where = piece(chunk, my_z)
            center[par, where, :] = updated
            spread_hop(par, chunk, 0, 1).start()
            spread_hop(par, chunk, 0, -1).start()
            return motion + in_rows((updated - center[old, where, :]) ** 2)

        motion = lax.fori_loop(0, CHUNKS, update, jnp.zeros((8, TARGETS), jnp.float32))
        stage_f(par)

        for hop in range(1, 4):

            def forward(chunk):
                spread_hop(par, chunk, hop - 1, 1).wait_recv()
                spread_hop(par, chunk, hop, 1).start()
                spread_hop(par, chunk, hop - 1, -1).wait_recv()
                if hop < 3:
                    spread_hop(par, chunk, hop, -1).start()

            each_chunk(forward)
            if hop == 1:
                fitted = (observed[...] + row_dual[...] + share_mean[par]) * (1.0 / 17)
                drift = share_mean[par] - fitted
                fitted_mean[...] = fitted
                row_dual[...] = row_dual[...] + drift
                spread_rows = in_rows(drift**2)
                pull(par)

        def finish(chunk, spread):
            spread_hop(par, chunk, 3, 1).wait_recv()
            rows = pl.ds(pl.multiple_of(chunk * CHUNK, CHUNK), CHUNK)
            new = center[par, rows, :]
            new_dual = summed[rows, :] - new
            dual[rows, :] = new_dual
            right_side[rows, :] = (new - new_dual + pulled[rows, :]).astype(jnp.bfloat16)
            return spread + in_rows((copies[rows, :] - new) ** 2)

        spread = lax.fori_loop(0, CHUNKS, finish, spread_rows)

        def sent(chunk):
            first_hop(par, chunk, 1).wait_send()
            first_hop(par, chunk, -1).wait_send()
            for slot, sign in ((1, 1), (2, 1), (3, 1), (5, -1), (6, -1)):
                next_hop(par, chunk, slot, sign).wait_send()
            y_swap(par, chunk).wait_send()
            for hop in range(4):
                spread_hop(par, chunk, hop, 1).wait_send()
            for hop in range(3):
                spread_hop(par, chunk, hop, -1).wait_send()

        each_chunk(sent)
        row = lax.broadcasted_iota(jnp.int32, (8, TARGETS), 0)
        lane = lax.broadcasted_iota(jnp.int32, (8, TARGETS), 1)
        spread_here = jnp.where((row == k) & (lane == 0), jnp.sum(spread), 0.0)
        motion_here = jnp.where((row == k) & (lane == 1), 8.0 * jnp.sum(motion), 0.0)
        record[...] = record[...] + (spread_here + motion_here)
        return carry

    lax.fori_loop(0, ITERS, iteration, 0)

    last = (ITERS - 1) % 2
    store = pltpu.make_async_copy(center.at[last], coef_hbm, store_sem)
    store.start()
    fitted_ref[...] = fitted_mean[...] * 16.0

    slot = 0
    for axis, size in (("rows_1", 8), ("rows_0", 2), ("cols_0", 4), ("cols_1", 2), ("cols_2", 2)):
        index = lax.axis_index(axis)
        swaps = []
        for step in range(1, size):
            there = lax.rem(index + step, size)
            arriving = lax.rem(index + size - step, size)
            swaps.append(
                (
                    remote(
                        record, record_in.at[slot + index], h_send.at[slot + step], h_recv.at[slot + index],
                        device(**{axis: there}),
                    ),
                    remote(
                        record, record_in.at[slot + arriving], h_send.at[slot + step], h_recv.at[slot + arriving],
                        device(**{axis: there}),
                    ),
                )
            )
        for going, coming in swaps:
            going.start()
        record_in[slot + index] = record[...]
        for going, coming in swaps:
            coming.wait_recv()
        for going, coming in swaps:
            going.wait_send()
        total = record_in[slot]
        for part in range(1, size):
            total = total + record_in[slot + part]
        record[...] = total
        slot += size
    history_ref[...] = record[0:ITERS, 0:2] * (1.0 / NORMALIZER)
    store.wait()


def local(matrix, inverse, target, penalty, consensus, copy_duals, fit_parts, fit_mean, fit_duals):
    f32, bf16 = jnp.float32, jnp.bfloat16
    anywhere = pl.BlockSpec(memory_space=pl.ANY)
    inside = pl.BlockSpec(memory_space=pltpu.VMEM)
    dma = pltpu.SemaphoreType.DMA

    def v(*shape, dtype=f32):
        return pltpu.VMEM(shape, dtype)

    return pl.pallas_call(
        kernel,
        name="admm",
        out_shape=(
            jax.ShapeDtypeStruct((WIDTH, TARGETS), f32),
            jax.ShapeDtypeStruct((HEIGHT, TARGETS), f32),
            jax.ShapeDtypeStruct((ITERS, 2), f32),
        ),
        in_specs=[anywhere, anywhere, anywhere, inside, anywhere, anywhere, anywhere, anywhere, anywhere],
        out_specs=(anywhere, inside, inside),
        scratch_shapes=[
            v(WIDTH, WIDTH, dtype=bf16),
            v(HEIGHT, WIDTH, dtype=bf16),
            v(WIDTH, HEIGHT, dtype=bf16),
            v(2, WIDTH, TARGETS),
            v(WIDTH, TARGETS),
            v(WIDTH, TARGETS),
            v(WIDTH, TARGETS),
            v(WIDTH, TARGETS),
            v(WIDTH, TARGETS, dtype=bf16),
            v(WIDTH, TARGETS, dtype=bf16),
            v(HEIGHT, TARGETS),
            v(2, HEIGHT, TARGETS),
            v(HEIGHT, TARGETS),
            v(HEIGHT, TARGETS),
            v(HEIGHT, TARGETS),
            v(2, CHUNKS, 7, PIECE, TARGETS),
            v(2, CHUNKS, PIECE, TARGETS),
            v(2, CHUNKS, PIECE, TARGETS),
            v(2, HALF, TARGETS),
            v(2, 3, QUARTER, TARGETS),
            v(HALF, TARGETS),
            v(QUARTER, TARGETS),
            v(2, QUARTER, TARGETS),
            v(8, TARGETS),
            v(18, 8, TARGETS),
            dma((LOADS,)),
            dma((CHUNKS,)),
            dma,
            dma((2, CHUNKS, 7)),
            dma((2, CHUNKS, 7)),
            dma((2, CHUNKS, 7)),
            dma((2, CHUNKS, 7)),
            dma((2, CHUNKS)),
            dma((2, CHUNKS)),
            dma((2, 9)),
            dma((2, 9)),
            dma((18,)),
            dma((18,)),
        ],
        compiler_params=pltpu.CompilerParams(
            collective_id=0, has_side_effects=True, vmem_limit_bytes=48 * 1024 * 1024
        ),
    )(inverse, matrix, target, penalty.reshape(1, TARGETS), consensus, copy_duals, fit_parts, fit_mean, fit_duals)


def solution(mesh):
    split = Mesh(mesh.devices.reshape(SIZES), AXES)
    return jax.shard_map(
        local,
        mesh=split,
        in_specs=(
            P(ROWS, COLS),
            P(ROWS, COLS),
            P(ROWS, None),
            P(),
            P(COLS, None),
            P(ROWS, COLS, None),
            P(COLS, ROWS, None),
            P(ROWS, None),
            P(ROWS, None),
        ),
        out_specs=(P(COLS, None), P(ROWS, None), P()),
        check_vma=False,
    )
```

time: 518 us -> 218 us (0.42)
  waiting for transfers between devices: 262 us -> 0 us
  Pallas kernels: 0 us -> 207 us
  starting transfers between devices: 74.1 us -> 0 us
  matrix products: 49.3 us -> 0 us
  blocking collectives: 43.5 us -> 0 us
  local copies, waits for them, and re-layouts: 38.9 us -> 10.2 us
  other arithmetic: 24.3 us -> 0 us
  between operations: 23.6 us -> 0.66 us
    pallas_call x0 -> x1, Pallas kernels: none -> 207 us  [local(): pl.pallas_call(kernel, name='admm', out_shape=(jax.ShapeDtypeStruct((WIDT...]
    all_to_all x11 -> x0, waiting for transfers between devices: 158 us -> none  [the longest x5 117 us: sum_at_owner(): tiles = lax.all_to_all(in_blocks(array, dim, count), axis, 0, 0, tiled=True)]
    all_gather x5 -> x0, waiting for transfers between devices: 104 us -> none  [gathered_total(): return lax.all_gather(array, axis).sum(0)]
    all_to_all x11 -> x0, starting transfers between devices: 73.5 us -> none  [the longest x6 39.9 us: sent_to_all(): lax.all_to_all(jnp.broadcast_to(array[None], (count, *array.shape)), axis...]
    dot_general x10 -> x0, matrix products: 49.3 us -> none  [the longest x5 41 us: local(): copies = jnp.dot(inverse, right_side, preferred_element_type=jnp.float32)]
    psum x5 -> x0, blocking collectives: 43.5 us -> none  [over_axes(): array = lax.psum(array, axis)]
    reduce_sum x19 -> x0, other arithmetic: 21.4 us -> none  [the longest x5 7.94 us: local(): motion = row_devices * jnp.sum((updated - old_rows) ** 2)]
    reshape x9 -> x0, local copies, waits for them, and re-layouts: 11.5 us -> none  [the longest x5 5.87 us: joined_along(): return jnp.moveaxis(tiles, 0, dim).reshape(shape)]
  transfers between devices with their start and end apart: 16 -> 0, of which waited for: 13 -> 0; matrix products, arithmetic and copies ran while one was open for 10% -> 0% of each run, Pallas kernels for 0% -> 0%
where the time goes in v1:
time: 218 us
  Pallas kernels  207 us (95%)
  local copies, waits for them, and re-layouts  10.2 us (5%)
    pallas_call x1, Pallas kernels, local(): pl.pallas_call(kernel, name='admm', out_shape=(jax.ShapeDtypeStruct((WIDT...  207 us
    unnamed x18, local copies, waits for them, and re-layouts  9.56 us

profile of v1, /device:TPU:1, one launch (start us, length us, event | category | flops | bytes accessed | tf_op | source)
XLA Modules:
  0.0 217.5 jit_solution(3206329745512619870)
XLA Ops:
  0.6 0.0 copy-start
  0.6 1.2 copy-done
  1.9 0.0 copy-start.1
  1.9 1.2 copy-done.1
  3.1 0.0 copy-start.2
  3.1 1.2 copy-done.2
  4.3 0.0 copy-start.3
  4.3 0.9 copy-done.3
  5.2 0.0 copy-start.4
  5.2 0.9 copy-done.4
  6.1 0.0 copy-start.5
  6.1 0.9 copy-done.5
  7.0 0.0 copy-start.6
  7.0 0.9 copy-done.6
  7.9 0.0 copy-start.7
  7.9 0.7 copy-done.7
  8.6 206.6 %admm.1 = (f32[2048,128]{1,0:T(8,128)S(1)}, f32[256,128]{1,0:T(8,128)S(1)}, f32[5,2]{1,0:T(8,128)S(1)}) custom-call(bf16[2048,2048]{1,0:T(8,128)(2,1)} %inverse_hbm.1, bf16[256,2048]{1,0:T(8,128)(2,1)S(1)} %copy-done, f32[256,128]{1,0:T(8,128)S(1)} %copy-done.3, f32[1,128]{1,0:T(1,128)S(1)} %bitcast.1, f32[2048,128]{1,0:T(8,128)S(1)} %copy-done.1, ...), custom_call_target="tpu_custom_call" | custom-call | tf_op jit(solution)/shard_map/admm/pallas_call | solution.py:392
  215.2 0.6 copy.12
  215.9 1.0 copy.15
  216.9 0.7 copy.16
Async XLA Ops:
  0.6 1.2 copy-start
  1.9 1.2 copy-start.1
  3.1 1.2 copy-start.2
  4.3 0.9 copy-start.3
  5.2 0.9 copy-start.4
  6.1 0.9 copy-start.5
  7.0 0.9 copy-start.6
  7.9 0.7 copy-start.7

commit v2 on v1

v2 whole, which is shorter than its diff:
```python
import jax
import jax.numpy as jnp
from jax import lax
from jax.experimental import pallas as pl
from jax.experimental.pallas import tpu as pltpu
from jax.sharding import Mesh
from jax.sharding import PartitionSpec as P

ITERS = 5
ROWS = ("rows_0", "rows_1")
COLS = ("cols_0", "cols_1", "cols_2")
AXES = ("rows_0", "rows_1", "cols_0", "cols_1", "cols_2")
SIZES = (2, 8, 4, 2, 2)
MESH = pl.DeviceIdType.MESH
GROUPS = (("cols_2",), ("rows_0",), ("cols_1",), ("cols_0",), ("rows_1",))

WIDTH = 2048
HEIGHT = 256
TARGETS = 128
NZ = 8
CHUNKS = 4
CHUNK = WIDTH // CHUNKS
PIECE = CHUNK // NZ
BLOCK = 512
SMALL = 512
HALF = HEIGHT // 2
QUARTER = HALF // 4
LOADS = 7
FIRST = {0: (1, 3, 1), 3: (-1, -3, 1), 6: (1, 4, 2)}
SPREAD = {0: (1, 0, 1), 1: (1, -1, 1), 2: (1, -2, 1), 3: (-1, 0, 1), 4: (-1, 1, 1), 5: (-1, 2, 1), 6: (1, -2, 2)}
NORMALIZER = 16.0 * 32768.0 * 128.0


def kernel(
    inverse_hbm, matrix_hbm, target_hbm, penalty_ref, consensus_hbm, duals_hbm, parts_hbm, mean_hbm, fit_duals_hbm,
    coef_hbm, fitted_ref, history_ref,
    cache, tile, tile_t, center, dual, summed, copies, pulled, right_side, rounded,
    share, share_mean, fitted_mean, row_dual, observed,
    chain, y_out, y_in, core_in, x_in, half_sum, quarter_sum, yh_in, clip_piece, spread_sum, tally, record, record_in,
    load_sem, cache_sem, store_sem,
    rs_send, rs_recv, ag_send, ag_recv, y_send, y_recv, s_send, s_recv, h_send, h_recv,
):
    me = tuple(lax.axis_index(axis) for axis in AXES)
    my_y, my_z, my_x, my_yh, my_core = me

    def device(**moved):
        return tuple(moved.get(axis, index) for axis, index in zip(AXES, me))

    def z_at(offset):
        return lax.rem(my_z + offset + 2 * NZ, NZ)

    core_peer = device(cols_2=1 - my_core)
    yh_peer = device(cols_1=1 - my_yh)
    y_peer = device(rows_0=1 - my_y)

    def x_peer(step):
        return device(cols_0=lax.rem(my_x + step, 4))

    def group(stage):
        axes = GROUPS[stage]
        size, index = 1, 0
        for axis in axes:
            extent = SIZES[AXES.index(axis)]
            size, index = size * extent, index * extent + me[AXES.index(axis)]
        members = {}
        for step in range(1, size):
            rest, moved = lax.rem(index + step, size), {}
            for axis in reversed(axes):
                extent = SIZES[AXES.index(axis)]
                moved[axis] = lax.rem(rest, extent)
                rest = lax.div(rest, extent)
            members[step] = device(**moved)
        return size, index, members

    peers = [peer for stage in range(len(GROUPS)) for peer in group(stage)[2].values()]
    barrier = pltpu.get_barrier_semaphore()
    for peer in peers:
        pl.semaphore_signal(barrier, inc=1, device_id=peer, device_id_type=MESH)

    loads = [
        pltpu.make_async_copy(src, dst, load_sem.at[index])
        for index, (src, dst) in enumerate(
            (
                (parts_hbm.at[0], share),
                (matrix_hbm, tile),
                (mean_hbm, fitted_mean),
                (fit_duals_hbm, row_dual),
                (consensus_hbm, center.at[1]),
                (duals_hbm.at[0], dual),
                (target_hbm, observed),
            )
        )
    ]
    for load in loads:
        load.start()

    def cache_load(chunk):
        rows = pl.ds(chunk * CHUNK, CHUNK)
        return pltpu.make_async_copy(inverse_hbm.at[rows], cache.at[rows], cache_sem.at[chunk])

    for chunk in range(CHUNKS):
        cache_load(chunk).start()

    def remote(src, dst, send, recv, where):
        return pltpu.make_async_remote_copy(
            src_ref=src, dst_ref=dst, send_sem=send, recv_sem=recv, device_id=where, device_id_type=MESH
        )

    mine = pl.ds(my_core * HALF, HALF)
    other = pl.ds((1 - my_core) * HALF, HALF)

    def quarter(x_index):
        return pl.ds(x_index * QUARTER, QUARTER)

    def piece_of_mean(x_index):
        return pl.ds(my_core * HALF + x_index * QUARTER, QUARTER)

    def core_sum(par):
        return remote(share.at[other], core_in.at[par], s_send.at[par, 0], s_recv.at[par, 0], core_peer)

    def x_sum(par, step):
        return remote(
            half_sum.at[quarter(lax.rem(my_x + step, 4))], x_in.at[par, step - 1],
            s_send.at[par, step], s_recv.at[par, step], x_peer(step),
        )

    def yh_sum(par):
        return remote(quarter_sum, yh_in.at[par], s_send.at[par, 4], s_recv.at[par, 4], yh_peer)

    def x_copy(par, step):
        return remote(
            share_mean.at[par, piece_of_mean(my_x)], share_mean.at[par, piece_of_mean(my_x)],
            s_send.at[par, 4 + step], s_recv.at[par, 4 + step], x_peer(step),
        )

    def core_copy(par):
        return remote(
            share_mean.at[par, mine], share_mean.at[par, mine], s_send.at[par, 8], s_recv.at[par, 8], core_peer
        )

    def stage_a(par):
        core_sum(par).start()

    def stage_b(par):
        core_sum(par).wait()
        half_sum[...] = share[mine, :] + core_in[par]
        for step in range(1, 4):
            x_sum(par, step).start()

    def stage_c(par):
        for step in range(1, 4):
            x_sum(par, step).wait()
        quarter_sum[...] = half_sum[quarter(my_x), :] + (x_in[par, 0] + x_in[par, 1] + x_in[par, 2])
        yh_sum(par).start()

    def stage_d(par):
        yh_sum(par).wait()
        share_mean[par, piece_of_mean(my_x), :] = (quarter_sum[...] + yh_in[par]) * (1.0 / 16)
        for step in range(1, 4):
            x_copy(par, step).start()

    def stage_e(par):
        for step in range(1, 4):
            x_copy(par, step).wait()
        core_copy(par).start()

    def stage_f(par):
        core_copy(par).wait()

    def pull(par):
        offsets = (share[...] - share_mean[par] + fitted_mean[...] - row_dual[...]).astype(jnp.bfloat16)
        pulled[...] = jnp.dot(tile_t[...], offsets, preferred_element_type=jnp.float32)

    loads[0].wait()
    pl.semaphore_wait(barrier, len(peers))
    stage_a(1)
    loads[1].wait()

    def transpose_block(block, carry):
        columns = pl.ds(pl.multiple_of(block * HEIGHT, HEIGHT), HEIGHT)
        tile_t[columns, :] = tile[:, columns].T
        return carry

    lax.fori_loop(0, WIDTH // HEIGHT, transpose_block, 0)
    stage_b(1)
    for load in loads[2:]:
        load.wait()
    record[...] = jnp.zeros_like(record)
    clip_piece[...] = jnp.zeros_like(clip_piece)
    stage_c(1)
    stage_d(1)
    stage_e(1)
    stage_f(1)
    pull(1)

    def first_right_side(block, carry):
        rows = pl.ds(pl.multiple_of(block * HEIGHT, HEIGHT), HEIGHT)
        right_side[rows, :] = (center[1, rows, :] - dual[rows, :] + pulled[rows, :]).astype(jnp.bfloat16)
        return carry

    lax.fori_loop(0, WIDTH // HEIGHT, first_right_side, 0)
    threshold = penalty_ref[...] * (1.0 / 16)
    for chunk in range(CHUNKS):
        cache_load(chunk).wait()

    z_near = {offset: z_at(offset) for offset in range(-4, 5)}
    z_device = {offset: device(rows_1=z_near[offset]) for offset in (-2, -1, 1, 2)}

    def turn(chunk):
        return 1 - 2 * (chunk % 2)

    def piece(chunk, offset):
        return pl.ds(pl.multiple_of(chunk * CHUNK + z_near[offset] * PIECE, PIECE), PIECE)

    def first_hop(par, chunk, slot):
        sign, far, hops = FIRST[slot]
        way = turn(chunk)
        return remote(
            summed.at[piece(chunk, far * way)], chain.at[par, chunk, slot],
            rs_send.at[par, chunk, slot], rs_recv.at[par, chunk, slot], z_device[sign * hops * way],
        )

    def next_hop(par, chunk, slot):
        sign = 1 if slot < 3 else -1
        return remote(
            chain.at[par, chunk, slot - 1], chain.at[par, chunk, slot],
            rs_send.at[par, chunk, slot], rs_recv.at[par, chunk, slot], z_device[sign * turn(chunk)],
        )

    def add_here(par, chunk, slot, offset):
        total = chain[par, chunk, slot] + summed[piece(chunk, offset * turn(chunk)), :]
        chain[par, chunk, slot] = total if slot > 0 else total + chain[par, chunk, 6]

    def y_swap(par, chunk):
        return remote(y_out.at[par, chunk], y_in.at[par, chunk], y_send.at[par, chunk], y_recv.at[par, chunk], y_peer)

    def spread_hop(par, chunk, slot):
        sign, owner, hops = SPREAD[slot]
        way = turn(chunk)
        where = piece(chunk, owner * way)
        return remote(
            center.at[par, where], center.at[par, where],
            ag_send.at[par, chunk, slot], ag_recv.at[par, chunk, slot], z_device[sign * hops * way],
        )

    def in_rows(values):
        return jnp.sum(values.reshape(-1, 8, TARGETS), axis=0)

    def chunk_rows(chunk):
        return slice(chunk * CHUNK, (chunk + 1) * CHUNK)

    def note(row, lane, value):
        rows = lax.broadcasted_iota(jnp.int32, (8, TARGETS), 0)
        lanes = lax.broadcasted_iota(jnp.int32, (8, TARGETS), 1)
        record[...] = record[...] + jnp.where((rows == row) & (lanes == lane), jnp.sum(value), 0.0)

    first_slot = (0, 2, 4, 6, 10)

    def record_swaps(stage):
        slot = first_slot[stage]
        size, index, members = group(stage)
        swaps = []
        for step in range(1, size):
            arriving = lax.rem(index + size - step, size)
            swaps.append(
                tuple(
                    remote(
                        record, record_in.at[slot + at], h_send.at[slot + step], h_recv.at[slot + at], members[step]
                    )
                    for at in (index, arriving)
                )
            )
        return slot, size, index, swaps

    def record_start(stage):
        slot, size, index, swaps = record_swaps(stage)
        for going, coming in swaps:
            going.start()
        record_in[slot + index] = record[...]

    def record_finish(stage):
        slot, size, index, swaps = record_swaps(stage)
        for going, coming in swaps:
            coming.wait_recv()
        for going, coming in swaps:
            going.wait_send()
        total = record_in[slot]
        for part in range(1, size):
            total = total + record_in[slot + part]
        record[...] = total

    def first_hops(par, chunk):
        way = 1 - 2 * lax.rem(chunk, 2)
        for slot in (6, 0, 3):
            sign, far, hops = FIRST[slot]
            where = pl.ds(pl.multiple_of(chunk * CHUNK + z_at(far * way) * PIECE, PIECE), PIECE)
            remote(
                summed.at[where], chain.at[par, chunk, slot],
                rs_send.at[par, chunk, slot], rs_recv.at[par, chunk, slot], device(rows_1=z_at(sign * hops * way)),
            ).start()

    def sums_sent(par):
        for chunk in range(CHUNKS):
            for slot in (0, 3, 6):
                first_hop(par, chunk, slot).wait_send()
            for slot in (1, 2, 4, 5):
                next_hop(par, chunk, slot).wait_send()
            y_swap(par, chunk).wait_send()

    def copies_sent(par):
        for chunk in range(CHUNKS):
            for slot in range(7):
                spread_hop(par, chunk, slot).wait_send()

    def iteration(k, carry):
        par = lax.rem(k, 2)
        old = 1 - par
        last = k == ITERS - 1
        zeros = jnp.zeros((8, TARGETS), jnp.float32)

        def multiply(chunk, carry):
            def block_of_chunk(block, carry):
                rows = pl.ds(pl.multiple_of(chunk * CHUNK + block * BLOCK, BLOCK), BLOCK)
                product = jnp.dot(cache[rows, :], right_side[...], preferred_element_type=jnp.float32)
                copies[rows, :] = product
                rounded[rows, :] = product.astype(jnp.bfloat16)
                summed[rows, :] = product + dual[rows, :]
                return carry

            lax.fori_loop(0, CHUNK // BLOCK, block_of_chunk, 0)
            first_hops(par, chunk)
            return carry

        lax.fori_loop(0, CHUNKS, multiply, 0)
        share[...] = jnp.dot(tile[...], rounded[...], preferred_element_type=jnp.float32)
        stage_a(par)


        for chunk in range(CHUNKS):
            first_hop(par, chunk, 3).wait_recv()
            add_here(par, chunk, 3, -2)
            next_hop(par, chunk, 4).start()
            first_hop(par, chunk, 0).wait_recv()
            first_hop(par, chunk, 6).wait_recv()
            add_here(par, chunk, 0, 2)
            next_hop(par, chunk, 1).start()
            if chunk == 1:
                stage_b(par)


        @pl.when(last)
        def _():
            def from_old(block, total):
                rows = pl.ds(pl.multiple_of(block * HEIGHT, HEIGHT), HEIGHT)
                return total + in_rows((copies[rows, :] - center[old, rows, :]) ** 2)

            spread_sum[...] = lax.fori_loop(0, WIDTH // HEIGHT, from_old, zeros)
            for row in range(ITERS - 1):
                for lane in range(2):
                    note(row, lane, tally[row, lane])

        for chunk in range(CHUNKS):
            next_hop(par, chunk, 4).wait_recv()
            add_here(par, chunk, 4, -1)
            next_hop(par, chunk, 5).start()
            next_hop(par, chunk, 1).wait_recv()
            add_here(par, chunk, 1, 1)
            next_hop(par, chunk, 2).start()
            if chunk == 1:
                stage_c(par)


        @pl.when(k > 0)
        def _():
            copies_sent(old)

        for chunk in range(CHUNKS):
            next_hop(par, chunk, 5).wait_recv()
            next_hop(par, chunk, 2).wait_recv()
            y_out[par, chunk] = summed[piece(chunk, 0), :] + (chain[par, chunk, 2] + chain[par, chunk, 5])
            y_swap(par, chunk).start()
            if chunk == 1:
                stage_d(par)


        def record_step(stage):
            @pl.when(last)
            def _():
                record_finish(stage)
                record_start(stage + 1)

        motion = shift = zeros
        for chunk in range(CHUNKS):
            y_swap(par, chunk).wait_recv()
            average = (y_out[par, chunk] + y_in[par, chunk]) * (1.0 / 16)
            clipped = jnp.clip(average, -threshold, threshold)
            updated = average - clipped
            where = piece(chunk, 0)
            center[par, where, :] = updated
            spread_hop(par, chunk, 0).start()
            spread_hop(par, chunk, 3).start()
            before = center[old, where, :]
            moved = updated - before
            if chunk == 1:
                stage_e(par)
            motion = motion + in_rows(moved**2)
            ahead = average - clip_piece[chunk] - before
            shift = shift + in_rows(moved * (8.0 * moved - 16.0 * ahead))
            clip_piece[chunk] = clipped
        tally[k, 1] = 8.0 * motion
        sums_sent(par)

        for chunk in range(CHUNKS):
            for slot in (0, 3):
                spread_hop(par, chunk, slot).wait_recv()
                spread_hop(par, chunk, slot + 1).start()
        stage_f(par)
        fitted = (observed[...] + row_dual[...] + share_mean[par]) * (1.0 / 17)
        drift = share_mean[par] - fitted
        drift_sum = in_rows(drift**2)

        @pl.when(last)
        def _():
            note(ITERS - 1, 0, spread_sum[...] + (shift + drift_sum))
            note(ITERS - 1, 1, tally[ITERS - 1, 1])
            record_start(0)
            fitted_ref[...] = fitted * 16.0

        @pl.when(k < ITERS - 1)
        def _():
            fitted_mean[...] = fitted
            row_dual[...] = row_dual[...] + drift
            pull(par)

        for chunk in range(CHUNKS):
            spread_hop(par, chunk, 1).wait_recv()
            spread_hop(par, chunk, 6).start()
            spread_hop(par, chunk, 2).start()
            spread_hop(par, chunk, 4).wait_recv()
            spread_hop(par, chunk, 5).start()
            if chunk % 2 == 1:
                record_step(chunk // 2)

        for chunk in range(CHUNKS):
            spread_hop(par, chunk, 2).wait_recv()
            spread_hop(par, chunk, 5).wait_recv()
            spread_hop(par, chunk, 6).wait_recv()
            if chunk == 1:
                record_step(2)
            rows = chunk_rows(chunk)

            @pl.when(last)
            def _():
                pltpu.make_async_copy(center.at[par, rows], coef_hbm.at[rows], store_sem.at[chunk]).start()

            @pl.when(k < ITERS - 1)
            def _():
                def settle(block, part):
                    rows = pl.ds(pl.multiple_of(chunk * CHUNK + block * SMALL, SMALL), SMALL)
                    new = center[par, rows, :]
                    new_dual = summed[rows, :] - new
                    dual[rows, :] = new_dual
                    right_side[rows, :] = (new - new_dual + pulled[rows, :]).astype(jnp.bfloat16)
                    return part + in_rows((copies[rows, :] - new) ** 2)

                part = lax.fori_loop(0, CHUNK // SMALL, settle, zeros)
                spread_sum[...] = (drift_sum if chunk == 0 else spread_sum[...]) + part

        @pl.when(last)
        def _():
            record_finish(3)
            record_start(4)

        tally[k, 0] = spread_sum[...]

        return carry

    lax.fori_loop(0, ITERS, iteration, 0)
    copies_sent((ITERS - 1) % 2)
    record_finish(4)
    history_ref[...] = record[0:ITERS, 0:2] * (1.0 / NORMALIZER)
    for chunk in range(CHUNKS):
        rows = chunk_rows(chunk)
        pltpu.make_async_copy(center.at[(ITERS - 1) % 2, rows], coef_hbm.at[rows], store_sem.at[chunk]).wait()


def local(matrix, inverse, target, penalty, consensus, copy_duals, fit_parts, fit_mean, fit_duals):
    f32, bf16 = jnp.float32, jnp.bfloat16
    anywhere = pl.BlockSpec(memory_space=pltpu.HBM)
    inside = pl.BlockSpec(memory_space=pltpu.VMEM)
    dma = pltpu.SemaphoreType.DMA

    def v(*shape, dtype=f32):
        return pltpu.VMEM(shape, dtype)

    return pl.pallas_call(
        kernel,
        name="admm",
        out_shape=(
            jax.ShapeDtypeStruct((WIDTH, TARGETS), f32),
            jax.ShapeDtypeStruct((HEIGHT, TARGETS), f32),
            jax.ShapeDtypeStruct((ITERS, 2), f32),
        ),
        in_specs=[anywhere, anywhere, anywhere, inside, anywhere, anywhere, anywhere, anywhere, anywhere],
        out_specs=(anywhere, inside, inside),
        scratch_shapes=[
            v(WIDTH, WIDTH, dtype=bf16),
            v(HEIGHT, WIDTH, dtype=bf16),
            v(WIDTH, HEIGHT, dtype=bf16),
            v(2, WIDTH, TARGETS),
            v(WIDTH, TARGETS),
            v(WIDTH, TARGETS),
            v(WIDTH, TARGETS),
            v(WIDTH, TARGETS),
            v(WIDTH, TARGETS, dtype=bf16),
            v(WIDTH, TARGETS, dtype=bf16),
            v(HEIGHT, TARGETS),
            v(2, HEIGHT, TARGETS),
            v(HEIGHT, TARGETS),
            v(HEIGHT, TARGETS),
            v(HEIGHT, TARGETS),
            v(2, CHUNKS, 7, PIECE, TARGETS),
            v(2, CHUNKS, PIECE, TARGETS),
            v(2, CHUNKS, PIECE, TARGETS),
            v(2, HALF, TARGETS),
            v(2, 3, QUARTER, TARGETS),
            v(HALF, TARGETS),
            v(QUARTER, TARGETS),
            v(2, QUARTER, TARGETS),
            v(CHUNKS, PIECE, TARGETS),
            v(8, TARGETS),
            v(ITERS, 2, 8, TARGETS),
            v(8, TARGETS),
            v(18, 8, TARGETS),
            dma((LOADS,)),
            dma((CHUNKS,)),
            dma((CHUNKS,)),
            dma((2, CHUNKS, 7)),
            dma((2, CHUNKS, 7)),
            dma((2, CHUNKS, 7)),
            dma((2, CHUNKS, 7)),
            dma((2, CHUNKS)),
            dma((2, CHUNKS)),
            dma((2, 9)),
            dma((2, 9)),
            dma((18,)),
            dma((18,)),
        ],
        compiler_params=pltpu.CompilerParams(
            collective_id=0, has_side_effects=True, vmem_limit_bytes=60 * 1024 * 1024
        ),
    )(inverse, matrix, target, penalty.reshape(1, TARGETS), consensus, copy_duals, fit_parts, fit_mean, fit_duals)


def solution(mesh):
    split = Mesh(mesh.devices.reshape(SIZES), AXES)
    return jax.shard_map(
        local,
        mesh=split,
        in_specs=(
            P(ROWS, COLS),
            P(ROWS, COLS),
            P(ROWS, None),
            P(),
            P(COLS, None),
            P(ROWS, COLS, None),
            P(COLS, ROWS, None),
            P(ROWS, None),
            P(ROWS, None),
        ),
        out_specs=(P(COLS, None), P(ROWS, None), P()),
        check_vma=False,
    )
```

time: 218 us -> 189 us (0.87)
  Pallas kernels: 207 us -> 182 us
  local copies, waits for them, and re-layouts: 10.2 us -> 5.14 us
    pallas_call x1, Pallas kernels: 207 us -> 182 us  [local(): pl.pallas_call(kernel, name='admm', out_shape=(jax.ShapeDtypeStruct((WIDT...]
    unnamed x18 -> x2, local copies, waits for them, and re-layouts: 9.56 us -> 3.83 us
where the time goes in v2:
time: 189 us; the launch traced here: 188 us
  Pallas kernels  182 us (96%)
  local copies, waits for them, and re-layouts  5.14 us (3%)
    pallas_call x1, Pallas kernels, local(): pl.pallas_call(kernel, name='admm', out_shape=(jax.ShapeDtypeStruct((WIDT...  182 us
    unnamed x2, local copies, waits for them, and re-layouts  3.83 us

profile of v2, /device:TPU:1, one launch (start us, length us, event | category | flops | bytes accessed | tf_op | source)
XLA Modules:
  0.0 187.5 jit_solution(10955425257209589912)
XLA Ops:
  0.6 181.8 %admm.1 = (f32[2048,128]{1,0:T(8,128)}, f32[256,128]{1,0:T(8,128)}, f32[5,2]{1,0:T(8,128)}) custom-call(bf16[2048,2048]{1,0:T(8,128)(2,1)} %inverse_hbm.1, bf16[256,2048]{1,0:T(8,128)(2,1)} %matrix_hbm.1, f32[256,128]{1,0:T(8,128)} %target_hbm.1, f32[1,128]{1,0:T(1,128)} %bitcast.1, f32[2048,128]{1,0:T(8,128)} %consensus_hbm.1, f32[1,2048,128]{2,1,0:T(8,128)} %duals_hbm.1, ...), custom_call_target="tpu_custom_call" | custom-call | tf_op jit(solution)/shard_map/admm/pallas_call | solution.py:496
  182.4 1.3 copy.12
  183.7 2.3 %copy.15 = f32[2048,128]{1,0:T(8,128)} copy(f32[2048,128]{1,0:T(8,128)} %get-tuple-element.9) | data formatting | bytes 2097152
  186.0 1.6 copy.16

commit v3 on v2

--- a/solution.py
+++ b/solution.py
@@ -174,6 +174,7 @@
     loads[0].wait()
     pl.semaphore_wait(barrier, len(peers))
     stage_a(1)
+    stage_b(1)
     loads[1].wait()
 
     def transpose_block(block, carry):
@@ -182,12 +183,11 @@
         return carry
 
     lax.fori_loop(0, WIDTH // HEIGHT, transpose_block, 0)
-    stage_b(1)
+    stage_c(1)
     for load in loads[2:]:
         load.wait()
     record[...] = jnp.zeros_like(record)
     clip_piece[...] = jnp.zeros_like(clip_piece)
-    stage_c(1)
     stage_d(1)
     stage_e(1)
     stage_f(1)
@@ -426,12 +426,6 @@
             record_start(0)
             fitted_ref[...] = fitted * 16.0
 
-        @pl.when(k < ITERS - 1)
-        def _():
-            fitted_mean[...] = fitted
-            row_dual[...] = row_dual[...] + drift
-            pull(par)
-
         for chunk in range(CHUNKS):
             spread_hop(par, chunk, 1).wait_recv()
             spread_hop(par, chunk, 6).start()
@@ -440,6 +434,12 @@
             spread_hop(par, chunk, 5).start()
             if chunk % 2 == 1:
                 record_step(chunk // 2)
+
+        @pl.when(k < ITERS - 1)
+        def _():
+            fitted_mean[...] = fitted
+            row_dual[...] = row_dual[...] + drift
+            pull(par)
 
         for chunk in range(CHUNKS):
             spread_hop(par, chunk, 2).wait_recv()

time: 189 us -> 188 us (level)
  Pallas kernels: 182 us -> 180 us
where the time goes in v3:
time: 188 us; the launch traced here: 186 us
  Pallas kernels  180 us (96%)
  local copies, waits for them, and re-layouts  5.14 us (3%)
    pallas_call x1, Pallas kernels, local(): pl.pallas_call(kernel, name='admm', out_shape=(jax.ShapeDtypeStruct((WIDT...  180 us
    unnamed x2, local copies, waits for them, and re-layouts  3.83 us

profile of v3, /device:TPU:1, one launch (start us, length us, event | category | flops | bytes accessed | tf_op | source)
XLA Modules:
  0.0 186.2 jit_solution(8019293814428935321)
XLA Ops:
  0.6 180.4 %admm.1 = (f32[2048,128]{1,0:T(8,128)}, f32[256,128]{1,0:T(8,128)}, f32[5,2]{1,0:T(8,128)}) custom-call(bf16[2048,2048]{1,0:T(8,128)(2,1)} %inverse_hbm.1, bf16[256,2048]{1,0:T(8,128)(2,1)} %matrix_hbm.1, f32[256,128]{1,0:T(8,128)} %target_hbm.1, f32[1,128]{1,0:T(1,128)} %bitcast.1, f32[2048,128]{1,0:T(8,128)} %consensus_hbm.1, f32[1,2048,128]{2,1,0:T(8,128)} %duals_hbm.1, ...), custom_call_target="tpu_custom_call" | custom-call | tf_op jit(solution)/shard_map/admm/pallas_call | solution.py:496
  181.0 1.3 copy.12
  182.3 2.3 %copy.15 = f32[2048,128]{1,0:T(8,128)} copy(f32[2048,128]{1,0:T(8,128)} %get-tuple-element.9) | data formatting | bytes 2097152
  184.6 1.6 copy.16
